TPU v7x, 32 devices: a whole 2x2x4 slice. The times are simulated.
32 devices in a mesh: sample: 8 (over y, x, core), chan: 4 (over z).
Axes of the slice: x: 2, y: 2, z: 4, core: 2. Of those that a mesh axis runs over, the one named last changes fastest.
Arguments:
- snapshots: bfloat16 [8, 256, 512], P('sample', None, 'chan'), may hold values from -6 to 6
- first_weight: bfloat16 [256, 27, 256], P('chan'), may hold values from -0.078125 to 0.078125
- second_weight: bfloat16 [256, 27, 256], P('chan'), may hold values from -0.078125 to 0.078125
- cotangent: bfloat16 [8, 256, 512], P('sample', 'chan'), may hold values from -0.09375 to 0.09375
Outputs:
- second_out: bfloat16 [8, 256, 512], P('sample', 'chan')
- first_grad: float32 [256, 27, 256], P('chan', None, 'sample')
- second_grad: float32 [256, 27, 256], P('chan', None, 'sample')
All inputs are finite; a program needn't handle non-finite values.
Results may differ from a plain program's by a relative error of at most 0.0061.
Values may be sent and summed in bfloat16 or wider, within the bound.
No kernel may reach another device: no remote copies, remote signals or barrier semaphores. Data moves between devices by JAX's collectives and lax.ppermute only.
A program may use at most 128 MiB of HBM per device.

v0:
```python
import jax
import jax.numpy as jnp
from jax import lax
from jax.sharding import PartitionSpec as P

SIDE = 8


def shifted(fields):
    batch_size, channels = (fields.shape[0], fields.shape[1])
    cube_form = fields.reshape(batch_size, channels, SIDE, SIDE, SIDE)
    padded = jnp.pad(cube_form, ((0, 0), (0, 0), (1, 1), (1, 1), (1, 1)))
    shifted_views = []
    for tap_index in range(27):
        shift_depth, shift_rows, shift_cols = (tap_index // 9, tap_index // 3 % 3, tap_index % 3)
        shifted_views.append(
            padded[
                :,
                :,
                shift_depth : shift_depth + SIDE,
                shift_rows : shift_rows + SIDE,
                shift_cols : shift_cols + SIDE,
            ]
        )
    return jnp.stack(shifted_views, axis=2).reshape(batch_size, channels * 27, SIDE * SIDE * SIDE)


def spread(terms):
    batch_size, channels = (terms.shape[0], terms.shape[1] // 27)
    cube_form = terms.reshape(batch_size, channels, 27, SIDE, SIDE, SIDE)
    padded = jnp.pad(cube_form, ((0, 0), (0, 0), (0, 0), (1, 1), (1, 1), (1, 1)))
    total = jnp.zeros((batch_size, channels, SIDE, SIDE, SIDE), jnp.float32)
    for tap_index in range(27):
        shift_depth, shift_rows, shift_cols = (tap_index // 9, tap_index // 3 % 3, tap_index % 3)
        total = (
            total
            + padded[
                :,
                :,
                tap_index,
                2 - shift_depth : 2 - shift_depth + SIDE,
                2 - shift_rows : 2 - shift_rows + SIDE,
                2 - shift_cols : 2 - shift_cols + SIDE,
            ]
        )
    return total.reshape(batch_size, channels, SIDE * SIDE * SIDE)


def layer_sums(kernel_rows, patches):
    partial_value = jnp.einsum(
        "kc,bkp->bcp", kernel_rows, patches, preferred_element_type=jnp.float32
    )
    return lax.psum_scatter(partial_value, "chan", scatter_dimension=1, tiled=True)


def all_channels(grad_maps):
    return lax.all_gather(grad_maps, "chan", axis=1, tiled=True)


def body(snapshots, first_weight, second_weight, cotangent):
    channel_maps = lax.all_to_all(snapshots, "chan", split_axis=1, concat_axis=2, tiled=True)
    input_patches = shifted(channel_maps)
    first_rows = first_weight.reshape(-1, first_weight.shape[2])
    second_rows = second_weight.reshape(-1, second_weight.shape[2])
    first_sum = layer_sums(first_rows, input_patches)
    first_map = first_sum.astype(jnp.bfloat16)
    first_values = first_map.astype(jnp.float32)
    hidden = jax.nn.silu(first_values).astype(jnp.bfloat16)
    hidden_patches = shifted(hidden)
    second_out = layer_sums(second_rows, hidden_patches).astype(jnp.bfloat16)
    full_cotangent = all_channels(cotangent)
    second_term = jnp.einsum(
        "bkp,bcp->kc", hidden_patches, full_cotangent, preferred_element_type=jnp.float32
    )
    terms = jnp.einsum(
        "kc,bcp->bkp", second_rows, full_cotangent, preferred_element_type=jnp.float32
    )
    hidden_grad = spread(terms)
    sigmoid_values = jax.nn.sigmoid(first_values)
    first_map_grad = (
        hidden_grad * sigmoid_values * (1.0 + first_values * (1.0 - sigmoid_values))
    ).astype(jnp.bfloat16)
    full_map_grad = all_channels(first_map_grad)
    first_term = jnp.einsum(
        "bkp,bcp->kc", input_patches, full_map_grad, preferred_element_type=jnp.float32
    )
    first_grad, second_grad = (
        lax.psum_scatter(first_term, "sample", scatter_dimension=1, tiled=True),
        lax.psum_scatter(second_term, "sample", scatter_dimension=1, tiled=True),
    )
    return (
        second_out,
        first_grad.reshape(first_weight.shape[0], 27, -1),
        second_grad.reshape(second_weight.shape[0], 27, -1),
    )


def solution(mesh):
    placed = (
        P("sample", None, "chan"),
        P("chan", None, None),
        P("chan", None, None),
        P("sample", "chan", None),
    )
    return jax.shard_map(
        body,
        mesh=mesh,
        in_specs=placed,
        out_specs=(P("sample", "chan", None), P("chan", None, "sample"), P("chan", None, "sample")),
        check_vma=False,
    )
```

profile of v0, /device:TPU:0, one launch (start us, length us, event | category | flops | bytes accessed | tf_op | source)
XLA Modules:
  0.0 640.3 jit_solution(11114681304338015524)
XLA Ops:
  10.3 6.3 all-to-all-start
  16.7 1.7 copy.63
  19.5 14.5 %all_gather.6 = bf16[1,256,512]{2,1,0:T(8,128)(2,1)S(1)} all-gather(bf16[1,64,512]{2,1,0:T(8,128)(2,1)S(1)} %copy-done.4), channel_id=1, replica_groups=mesh['sample'=8,'chan'=4] {'chan'}, dimensions={1}, use_global_device_ids=true | all-gather | bytes 327680 | tf_op jit(solution)/shard_map/all_gather | solution.py:57
  34.7 1.8 convolution_bitcast_fusion
  36.5 3.1 copy.65
  39.6 22.4 %reshape.413 = f32[1,64,27,8,8,8]{2,1,5,4,3,0:T(8,128)} reshape(f32[1,1728,512]{1,2,0:T(8,128)} %copy.65) | data formatting | bytes 7077888 | tf_op jit(solution)/shard_map/reshape | solution.py:30
  62.0 178.1 %fusion.16 = (f32[64,8,8,8]{0,3,2,1:T(8,128)S(1)}, f32[64,8,8,8]{0,3,2,1:T(8,128)S(1)}, f32[64,8,8,8]{0,3,2,1:T(8,128)S(1)}, f32[64,8,8,8]{0,3,2,1:T(8,128)S(1)}...) fusion(f32[1,64,27,8,8,8]{2,1,5,4,3,0:T(8,128)} %reshape.413), kind=kLoop, calls=%fused_computation.42 | loop fusion | flops 524288 | bytes 34996224 | tf_op jit(solution)/shard_map/slice | solution.py:37
  240.6 1.2 reshape.408
  262.6 9.5 %copy.58 = bf16[1,64,27,8,8,8]{2,1,5,4,3,0:T(8,128)(2,1)} copy(bf16[1,64,27,8,8,8]{1,5,4,3,2,0:T(8,128)(2,1)} %fusion.90) | data formatting | bytes 3538944 | tf_op jit(solution)/shard_map/stack | solution.py:25
  272.1 11.3 %reshape.407 = bf16[1728,512]{0,1:T(8,128)(2,1)S(1)} reshape(bf16[1,64,27,8,8,8]{2,1,5,4,3,0:T(8,128)(2,1)} %copy.58) | data formatting | bytes 3538944 | tf_op jit(solution)/shard_map/reshape.2
  283.4 2.6 convolution_bitcast_fusion.2
  286.0 1.3 copy.60
  287.3 140.8 %all-reduce.7 = bf16[1,256,512]{2,0,1:T(2,128)(2,1)} all-reduce(f32[1,256,512]{2,0,1:T(1,128)S(1)} %copy.60), channel_id=2, replica_groups=mesh['sample'=8,'chan'=4] {'chan'}, use_global_device_ids=true, to_apply=%region_0.1.clone | all-reduce | flops 131072 | bytes 786432
  429.3 1.6 fusion.33
  435.1 14.1 %all_gather.7 = bf16[1,256,512]{2,1,0:T(8,128)(2,1)S(1)} all-gather(bf16[1,64,512]{2,1,0:T(8,128)(2,1)S(1)} %copy.66), channel_id=1, replica_groups=mesh['sample'=8,'chan'=4] {'chan'}, dimensions={1}, use_global_device_ids=true | all-gather | bytes 327680 | tf_op jit(solution)/shard_map/all_gather | solution.py:57
  449.2 2.0 fusion.34
  465.7 9.6 %copy.62 = bf16[1,64,27,8,8,8]{2,1,5,4,3,0:T(8,128)(2,1)} copy(bf16[1,64,27,8,8,8]{1,5,4,3,2,0:T(8,128)(2,1)} %fusion.142) | data formatting | bytes 3538944 | tf_op jit(solution)/shard_map/stack | solution.py:25
  475.2 11.3 %reshape.410 = bf16[1728,512]{0,1:T(8,128)(2,1)S(1)} reshape(bf16[1,64,27,8,8,8]{2,1,5,4,3,0:T(8,128)(2,1)} %copy.62) | data formatting | bytes 3538944 | tf_op jit(solution)/shard_map/reshape.5
  486.6 1.9 fusion.37
  489.6 136.3 %all-reduce.8 = bf16[1,256,512]{2,0,1:T(2,128)(2,1)S(1)} all-reduce(f32[1,256,512]{2,0,1:T(1,128)S(1)} %copy.64), channel_id=3, replica_groups=mesh['sample'=8,'chan'=4] {'chan'}, use_global_device_ids=true, to_apply=%region_1.2.clone | all-reduce | flops 131072 | bytes 786432
  626.7 2.2 reshape.415
  628.9 1.2 copy.68
  630.1 2.2 reshape.416
  632.3 1.2 copy.69
  (90 shorter events, 47.3 us)
Async XLA Ops:
  7.2 12.4 %copy-start.4 = (bf16[1,64,512]{2,1,0:T(8,128)(2,1)S(1)}, bf16[1,64,512]{2,1,0:T(8,128)(2,1)}, u32[]{:S(2)}) copy-start(bf16[1,64,512]{2,1,0:T(8,128)(2,1)} %param.7) | copy-start | bytes 196612
  10.3 232.7 %all-to-all-start = ((bf16[4,2,4096]{2,1,0:T(2,128)(2,1)}), bf16[4,2,4096]{2,1,0:T(2,128)(2,1)}, u32[]{:S(2)}, u32[]{:S(2)}) async-start(bf16[4,2,4096]{2,1,0:T(2,128)(2,1)} %reshape.442), calls=%async_computation | async-start | bytes 131072 | tf_op jit(solution)/shard_map/all_to_all | solution.py:61
  16.6 610.1 %reduce-scatter.3.cloned.1.call-start = ((), (), s32[]{:S(2)}) async-start(), calls=%async_computation.3 | async-start | bytes 2064384 | tf_op jit(solution)/shard_map/reduce_scatter | solution.py:88
  34.0 0.7 copy-start.1
  62.0 178.1 %copy-start.3 = (bf16[64,27,256]{2,0,1:T(8,128)(2,1)S(1)}, bf16[64,27,256]{2,0,1:T(8,128)(2,1)}, u32[]{:S(2)}) copy-start(bf16[64,27,256]{2,0,1:T(8,128)(2,1)} %param.5) | copy-start | bytes 2654212
  240.1 1.7 copy-start.5
  451.2 178.8 %reduce-scatter.5.cloned.1.call-start = ((), (), s32[]{:S(2)}) async-start(), calls=%async_computation.4 | async-start | bytes 2064384 | tf_op jit(solution)/shard_map/reduce_scatter | solution.py:89
  475.2 11.4 %copy-start.2 = (bf16[1,256,512]{2,1,0:T(8,128)(2,1)S(1)}, bf16[1,256,512]{2,1,0:T(8,128)(2,1)}, u32[]{:S(2)}) copy-start(bf16[1,256,512]{2,1,0:T(8,128)(2,1)} %copy-done.1) | copy-start | bytes 786436
  486.6 1.9 copy-start
Sparse Core Ops, SparseCore 0:
  451.4 40.2 reduce-scatter.2
  495.0 39.6 reduce-scatter.4
where the time goes:
time: 642 us; the launch traced here: 640 us
  blocking collectives  306 us (48%)
  other arithmetic  181 us (28%)
  local copies, waits for them, and re-layouts  124 us (19%)
  between operations  14.9 us (2%)
  matrix products  8.92 us (1%)
    unnamed x2, blocking collectives  277 us
    slice x1, other arithmetic, spread(): padded[:, :, tap_index, 2 - shift_depth:2 - shift_depth + SIDE, 2 - shift...  178 us
    unnamed x76, local copies, waits for them, and re-layouts  46.2 us
    all_gather x2, blocking collectives, all_channels(): return lax.all_gather(grad_maps, 'chan', axis=1, tiled=True)  28.6 us
    another operation x2, local copies, waits for them, and re-layouts  22.6 us
    reshape x1, local copies, waits for them, and re-layouts, spread(): cube_form = terms.reshape(batch_size, channels, 27, SIDE, SIDE, SIDE)  22.4 us
    another operation x4, local copies, waits for them, and re-layouts, shifted(): jnp.stack(shifted_views, axis=2)  20.4 us
  transfers between devices with their start and end apart: 3, of which 0 were waited for; matrix products, arithmetic and copies ran while one was open for 39% of the time, Pallas kernels for 0%

commit v1 on v0

--- a/solution.py
+++ b/solution.py
@@ -54,7 +54,24 @@
 
 
 def all_channels(grad_maps):
-    return lax.all_gather(grad_maps, "chan", axis=1, tiled=True)
+
+    def _find_slices(patch):
+        n_slots = jax.lax.axis_size("chan")
+        entries = [patch]
+        m = 1
+        while m < n_slots:
+            entries.append(
+                jax.lax.ppermute(
+                    entries[m - 1],
+                    axis_name="chan",
+                    perm=[(tick, (tick - 1) % n_slots) for tick in range(n_slots)],
+                )
+            )
+            m += 1
+        piece_out = jnp.concatenate(entries, axis=1)
+        return jnp.roll(piece_out, jax.lax.axis_index("chan") * patch.shape[1], axis=1)
+
+    return _find_slices(grad_maps)
 
 
 def body(snapshots, first_weight, second_weight, cotangent):

time: 642 us -> 622 us (0.969)
  blocking collectives: 306 us -> 278 us
  local copies, waits for them, and re-layouts: 124 us -> 103 us
  starting transfers between devices: 6.36 us -> 24.5 us
  waiting for transfers between devices: 0.04 us -> 11.3 us
    all_gather x2 -> x0, blocking collectives: 28.6 us -> none  [all_channels(): return lax.all_gather(grad_maps, 'chan', axis=1, tiled=True)]
    ppermute x0 -> x6, starting transfers between devices: none -> 18.1 us  [_find_slices(): jax.lax.ppermute(entries[m - 1], axis_name='chan', perm=[(tick, (tick - 1...]
    unnamed x76 -> x82, local copies, waits for them, and re-layouts: 46.2 us -> 29.2 us
    ppermute x0 -> x6, waiting for transfers between devices: none -> 11.2 us  [_find_slices(): jax.lax.ppermute(entries[m - 1], axis_name='chan', perm=[(tick, (tick - 1...]
  transfers between devices with their start and end apart: 3 -> 9, of which waited for: 0 -> 4; matrix products, arithmetic and copies ran while one was open for 39% -> 9% of each run, Pallas kernels for 0% -> 0%
where the time goes in v1:
time: 622 us; the launch traced here: 621 us
  blocking collectives  278 us (45%)
  other arithmetic  180 us (29%)
  local copies, waits for them, and re-layouts  103 us (17%)
  starting transfers between devices  24.5 us (4%)
  between operations  15 us (2%)
  waiting for transfers between devices  11.3 us (2%)
  matrix products  9.42 us (2%)
    unnamed x2, blocking collectives  278 us
    slice x1, other arithmetic, spread(): padded[:, :, tap_index, 2 - shift_depth:2 - shift_depth + SIDE, 2 - shift...  177 us
    unnamed x82, local copies, waits for them, and re-layouts  29.2 us
    another operation x2, local copies, waits for them, and re-layouts  22.6 us
    reshape x1, local copies, waits for them, and re-layouts, spread(): cube_form = terms.reshape(batch_size, channels, 27, SIDE, SIDE, SIDE)  22.4 us
    ppermute x6, starting transfers between devices, _find_slices(): jax.lax.ppermute(entries[m - 1], axis_name='chan', perm=[(tick, (tick - 1...  18.1 us
    another operation x4, local copies, waits for them, and re-layouts, shifted(): jnp.stack(shifted_views, axis=2)  17.6 us
  transfers between devices with their start and end apart: 9, of which 4 were waited for; matrix products, arithmetic and copies ran while one was open for 9% of the time, Pallas kernels for 0%

profile of v1, /device:TPU:0, one launch (start us, length us, event | category | flops | bytes accessed | tf_op | source)
XLA Modules:
  0.0 621.5 jit_solution(8211519301164974273)
XLA Ops:
  10.4 6.3 %all-to-all-start = ((bf16[4,2,4096]{2,1,0:T(2,128)(2,1)}), bf16[4,2,4096]{2,1,0:T(2,128)(2,1)S(1)}, u32[]{:S(2)}, u32[]{:S(2)}) async-start(bf16[4,2,4096]{2,1,0:T(2,128)(2,1)} %reshape.442), calls=%async_computation | async-start | bytes 131072 | tf_op jit(solution)/shard_map/all_to_all | solution.py:78
  16.7 3.8 collective-permute-start
  20.5 1.7 copy.63
  45.5 9.5 %copy.58 = bf16[1,64,27,8,8,8]{2,1,5,4,3,0:T(8,128)(2,1)} copy(bf16[1,64,27,8,8,8]{1,5,4,3,2,0:T(8,128)(2,1)} %fusion.104) | data formatting | bytes 3538944 | tf_op jit(solution)/shard_map/stack | solution.py:25
  55.0 11.3 %reshape.407 = bf16[1728,512]{0,1:T(8,128)(2,1)S(1)} reshape(bf16[1,64,27,8,8,8]{2,1,5,4,3,0:T(8,128)(2,1)} %copy.58) | data formatting | bytes 3538944 | tf_op jit(solution)/shard_map/reshape.2
  68.6 141.7 %all-reduce.7 = bf16[1,256,512]{2,0,1:T(2,128)(2,1)S(1)} all-reduce(f32[1,256,512]{2,0,1:T(1,128)S(1)} %copy.60), channel_id=2, replica_groups=mesh['sample'=8,'chan'=4] {'chan'}, use_global_device_ids=true, to_apply=%region_0.1.clone | all-reduce | flops 131072 | bytes 786432
  212.6 2.0 collective-permute-done.2
  216.7 1.8 convolution_bitcast_fusion
  218.5 3.3 copy.65
  221.8 22.4 %reshape.413 = f32[1,64,27,8,8,8]{2,1,5,4,3,0:T(8,128)} reshape(f32[1,1728,512]{1,2,0:T(8,128)} %copy.65) | data formatting | bytes 7077888 | tf_op jit(solution)/shard_map/reshape | solution.py:30
  244.2 176.8 %fusion.16 = (f32[64,8,8,8]{0,3,2,1:T(8,128)S(1)}, f32[64,8,8,8]{0,3,2,1:T(8,128)S(1)}, f32[64,8,8,8]{0,3,2,1:T(8,128)S(1)}, f32[64,8,8,8]{0,3,2,1:T(8,128)S(1)}...) fusion(f32[1,64,27,8,8,8]{2,1,5,4,3,0:T(8,128)} %reshape.413), kind=kLoop, calls=%fused_computation.42 | loop fusion | flops 524288 | bytes 34996224 | tf_op jit(solution)/shard_map/slice | solution.py:37
  423.3 7.4 %copy.62 = bf16[1,64,27,8,8,8]{2,1,5,4,3,0:T(8,128)(2,1)} copy(bf16[1,64,27,8,8,8]{1,5,4,3,2,0:T(8,128)(2,1)S(1)} %fusion.156) | data formatting | bytes 3538944 | tf_op jit(solution)/shard_map/stack | solution.py:25
  430.7 11.3 %reshape.410 = bf16[1728,512]{0,1:T(8,128)(2,1)S(1)} reshape(bf16[1,64,27,8,8,8]{2,1,5,4,3,0:T(8,128)(2,1)} %copy.62) | data formatting | bytes 3538944 | tf_op jit(solution)/shard_map/reshape.5
  442.1 1.9 fusion.159
  444.0 3.1 collective-permute-start.3
  447.2 3.6 collective-permute-done.3
  450.8 4.3 collective-permute-start.4
  455.1 3.0 collective-permute-done.4
  458.1 4.3 collective-permute-start.5
  462.4 2.5 collective-permute-done.5
  464.9 4.5 fusion.39
  470.5 136.6 %all-reduce.8 = bf16[1,256,512]{2,0,1:T(2,128)(2,1)S(1)} all-reduce(f32[1,256,512]{2,0,1:T(1,128)S(1)} %copy.64), channel_id=3, replica_groups=mesh['sample'=8,'chan'=4] {'chan'}, use_global_device_ids=true, to_apply=%region_1.2.clone | all-reduce | flops 131072 | bytes 786432
  607.9 2.2 reshape.416
  611.3 2.2 reshape.415
  (106 shorter events, 38.9 us)
Async XLA Ops:
  7.2 16.3 %copy-start.4 = (bf16[64,27,256]{2,0,1:T(8,128)(2,1)S(1)}, bf16[64,27,256]{2,0,1:T(8,128)(2,1)}, u32[]{:S(2)}) copy-start(bf16[64,27,256]{2,0,1:T(8,128)(2,1)} %param.7) | copy-start | bytes 2654212
  10.4 16.4 %all-to-all-start = ((bf16[4,2,4096]{2,1,0:T(2,128)(2,1)}), bf16[4,2,4096]{2,1,0:T(2,128)(2,1)S(1)}, u32[]{:S(2)}, u32[]{:S(2)}) async-start(bf16[4,2,4096]{2,1,0:T(2,128)(2,1)} %reshape.442), calls=%async_computation | async-start | bytes 131072 | tf_op jit(solution)/shard_map/all_to_all | solution.py:78
  16.7 591.2 %reduce-scatter.5.cloned.1.call-start = ((), (), s32[]{:S(2)}) async-start(), calls=%async_computation.4 | async-start | bytes 2064384 | tf_op jit(solution)/shard_map/reduce_scatter | solution.py:106
  16.7 8.8 %collective-permute-start = (bf16[1,64,512]{2,1,0:T(8,128)(2,1)}, bf16[1,64,512]{2,1,0:T(8,128)(2,1)S(1)}, u32[]{:S(2)}, u32[]{:S(2)}) collective-permute-start(bf16[1,64,512]{2,1,0:T(8,128)(2,1)} %param.9), channel_id=1, source_target_pairs={{0,3},{1,0},{2,1},{3,2},{4,7},{5,4},{6,5},{7,6},{8,11},{9,8},{10,9... | collective-permute-start | bytes 196616 | tf_op jit(solution)/shard_map/ppermute | solution.py:64
  20.5 3.8 copy-start.8
  25.5 184.8 %collective-permute-start.1 = (bf16[1,64,512]{2,1,0:T(8,128)(2,1)S(1)}, bf16[1,64,512]{2,1,0:T(8,128)(2,1)S(1)}, u32[]{:S(2)}, u32[]{:S(2)}) collective-permute-start(bf16[1,64,512]{2,1,0:T(8,128)(2,1)S(1)} %collective-permute-done), channel_id=1, source_target_pairs={{0,3},{1,0},{2,1},{3,2},{4,7},{5,4},{6,5},{7,6},{8,11},{9,8},{10,9... | collective-permute-start | bytes 196616 | tf_op jit(solution)/shard_map/ppermute | solution.py:64
  66.3 1.2 copy-start.3
  67.5 147.1 %copy-start.7 = (bf16[1,64,512]{2,1,0:T(8,128)(2,1)S(1)}, bf16[1,64,512]{2,1,0:T(8,128)(2,1)}, u32[]{:S(2)}) copy-start(bf16[1,64,512]{2,1,0:T(8,128)(2,1)} %param.9) | copy-start | bytes 196612
  210.3 4.3 collective-permute-start.2
  216.0 0.7 copy-start.1
  244.2 176.8 %copy-start.5 = (bf16[1,64,512]{1,2,0:T(8,128)(2,1)S(1)}, bf16[1,64,512]{1,2,0:T(8,128)(2,1)}, u32[]{:S(2)}) copy-start(bf16[1,64,512]{1,2,0:T(8,128)(2,1)} %copy.61) | copy-start | bytes 196612
  430.7 11.4 %copy-start.2 = (bf16[256,512]{1,0:T(8,128)(2,1)S(1)}, bf16[256,512]{1,0:T(8,128)(2,1)}, u32[]{:S(2)}) copy-start(bf16[256,512]{1,0:T(8,128)(2,1)} %copy-done.1) | copy-start | bytes 786436
  442.1 2.0 copy-start.6
  444.0 167.3 %reduce-scatter.3.cloned.1.call-start = ((), (), s32[]{:S(2)}) async-start(), calls=%async_computation.3 | async-start | bytes 2064384 | tf_op jit(solution)/shard_map/reduce_scatter | solution.py:105
  444.0 25.4 %copy-start = (bf16[1728,256]{1,0:T(8,128)(2,1)S(1)}, bf16[1728,256]{1,0:T(8,128)(2,1)}, u32[]{:S(2)}) copy-start(bf16[1728,256]{1,0:T(8,128)(2,1)} %reshape.411) | copy-start | bytes 2654212
  444.0 6.8 %collective-permute-start.3 = (bf16[1,64,512]{1,2,0:T(8,128)(2,1)S(1)}, bf16[1,64,512]{1,2,0:T(8,128)(2,1)S(1)}, u32[]{:S(2)}, u32[]{:S(2)}) collective-permute-start(bf16[1,64,512]{1,2,0:T(8,128)(2,1)S(1)} %copy-done.6), channel_id=1, source_target_pairs={{0,3},{1,0},{2,1},{3,2},{4,7},{5,4},{6,5},{7,6},{8,11},{9,8},{10,9... | collective-permute-start | bytes 196616 | tf_op jit(solution)/shard_map/ppermute | solution.py:64
  450.8 7.3 %collective-permute-start.4 = (bf16[1,64,512]{1,2,0:T(8,128)(2,1)S(1)}, bf16[1,64,512]{1,2,0:T(8,128)(2,1)S(1)}, u32[]{:S(2)}, u32[]{:S(2)}) collective-permute-start(bf16[1,64,512]{1,2,0:T(8,128)(2,1)S(1)} %collective-permute-done.3), channel_id=1, source_target_pairs={{0,3},{1,0},{2,1},{3,2},{4,7},{5,4},{6,5},{7,6},{8,11},{9,8},{10,9... | collective-permute-start | bytes 196616 | tf_op jit(solution)/shard_map/ppermute | solution.py:64
  458.1 6.8 %collective-permute-start.5 = (bf16[1,64,512]{1,2,0:T(8,128)(2,1)S(1)}, bf16[1,64,512]{1,2,0:T(8,128)(2,1)S(1)}, u32[]{:S(2)}, u32[]{:S(2)}) collective-permute-start(bf16[1,64,512]{1,2,0:T(8,128)(2,1)S(1)} %collective-permute-done.4), channel_id=1, source_target_pairs={{0,3},{1,0},{2,1},{3,2},{4,7},{5,4},{6,5},{7,6},{8,11},{9,8},{10,9... | collective-permute-start | bytes 196616 | tf_op jit(solution)/shard_map/ppermute | solution.py:64
Sparse Core Ops, SparseCore 0:
  444.1 40.4 reduce-scatter.4
  487.9 39.6 reduce-scatter.2
